TPU v7x, 32 devices: a whole 2x2x4 slice. The times are simulated.
32 devices in a mesh: row: 8 (over z, y), col: 4 (over x, core).
Axes of the slice: x: 2, y: 2, z: 4, core: 2. Of those that a mesh axis runs over, the one named last changes fastest.
Arguments:
- orbitals: float32 [2048, 28672], P(('row', 'col')), may hold values from -0.03125 to 0.03125
- applied: float32 [2048, 28672], P(('row', 'col')), may hold values from -6 to 6
Outputs:
- hamiltonian: float32 [2048, 2048], P('col', 'row')
- intersection: float32 [2048, 2048], P('col', 'row')
All inputs are finite; a program needn't handle non-finite values.
Results may differ from a plain program's by a relative error of at most 0.000098.
Values sent between devices are 32-bit elements; how exact they have to be, the bound alone decides.
A program may use at most 192 MiB of HBM per device.

v0:
```python
import jax
import jax.numpy as jnp
from jax import lax
from jax.sharding import PartitionSpec as P


def product(left, right):
    return lax.dot_general(
        left,
        right,
        (((1,), (1,)), ((), ())),
        precision=lax.Precision.HIGHEST,
        preferred_element_type=jnp.float32,
    )


def shards(orbitals, applied):
    mine_orb, mine_app = (
        lax.all_to_all(orbitals, "col", split_axis=1, concat_axis=0, tiled=True),
        lax.all_to_all(applied, "col", split_axis=1, concat_axis=0, tiled=True),
    )
    every_orb = lax.all_gather(mine_orb, "row", axis=0, tiled=True)
    ham_part = product(every_orb, mine_app)
    ovl_part = product(every_orb, mine_orb)
    hamiltonian, intersection = (
        lax.psum_scatter(ham_part, "col", scatter_dimension=0, tiled=True),
        lax.psum_scatter(ovl_part, "col", scatter_dimension=0, tiled=True),
    )
    return (hamiltonian, intersection)


def solution(mesh):
    placed = (P(("row", "col"), None), P(("row", "col"), None))
    return jax.shard_map(
        shards,
        mesh=mesh,
        in_specs=placed,
        out_specs=(P("col", "row"), P("col", "row")),
        check_vma=False,
    )
```

profile of v0, /device:TPU:0, one launch (start us, length us, event | category | flops | bytes accessed | tf_op | source)
XLA Modules:
  0.0 1351.8 jit_solution(10958616130281556997)
XLA Ops:
  7.2 0.0 all-gather.2.cloned.1.call-start
  7.2 3.9 copy.13
  11.1 86.2 %all_to_all.38 = f32[64,4,7168]{2,0,1:T(8,128)} all-to-all(f32[64,4,7168]{2,0,1:T(8,128)S(1)} %bitcast.21), channel_id=1, replica_groups=mesh['row'=8,'col'=4] {'col'}, dimensions={1} | all-to-all | bytes 14680064 | tf_op jit(solution)/shard_map/all_to_all | solution.py:19
  97.3 0.0 all-gather.2.cloned.1.call-update
  97.3 6.9 copy.12
  104.3 5.6 all-to-all-start.1
  109.9 0.0 reduce-scatter.5.cloned.1.call-start
  109.9 1098.2 %all-gather.2.cloned.1.call-done = f32[2048,7168]{1,0:T(8,128)} async-done(((f32[256,7168]{1,0:T(8,128)}), f32[2048,7168]{1,0:T(8,128)}) %all-gather.2.cloned.1.call-update) | async-done | bytes 58720272 | tf_op jit(solution)/shard_map/all_gather | solution.py:22
  1208.2 52.8 %fusion.1 = f32[2048,256]{1,0:T(8,128)} fusion(f32[2048,7168]{1,0:T(8,128)} %all-gather.2.cloned.1.call-done, f32[256,7168]{1,0:T(8,128)} %bitcast.19), kind=kOutput, calls=%fused_computation.3 | convolution fusion | flops 45097156608 | bytes 68157440 | tf_op jit(solution)/shard_map/dot_general | solution.py:8
  1261.0 0.0 reduce-scatter.5.cloned.1.call-update
  1261.0 0.0 reduce-scatter.3.cloned.1.call-start
  1261.0 0.0 all-to-all-done.1
  1261.0 52.9 %fusion = f32[2048,256]{1,0:T(8,128)} fusion(f32[2048,7168]{1,0:T(8,128)} %all-gather.2.cloned.1.call-done, f32[256,7168]{1,0:T(8,128)} %bitcast.3), kind=kOutput, calls=%fused_computation.2 | convolution fusion | flops 45097156608 | bytes 68157440 | tf_op jit(solution)/shard_map/dot_general | solution.py:8
  1313.9 0.0 reduce-scatter.3.cloned.1.call-update
  1314.0 0.0 reduce-scatter.5.cloned.1.call-done
  1314.0 31.3 %reduce-scatter.3.cloned.1.call-done = f32[512,256]{1,0:T(8,128)} async-done(((f32[2048,256]{1,0:T(8,128)}), f32[512,256]{1,0:T(8,128)}) %reduce-scatter.3.cloned.1.call-update) | async-done | bytes 524304 | tf_op jit(solution)/shard_map/reduce_scatter | solution.py:26
Async XLA Ops:
  7.2 1201.0 %all-gather.2.cloned.1.call-start = ((), (), s32[]{:S(2)}) async-start(), calls=%async_computation.4 | async-start | bytes 66060288 | tf_op jit(solution)/shard_map/all_gather | solution.py:22
  104.3 1156.8 %all-to-all-start.1 = ((f32[64,4,7168]{2,0,1:T(8,128)}), f32[64,4,7168]{2,0,1:T(8,128)}, u32[]{:S(2)}, u32[]{:S(2)}) async-start(f32[64,4,7168]{2,0,1:T(8,128)} %bitcast.20), calls=%async_computation.1 | async-start | bytes 14680064 | tf_op jit(solution)/shard_map/all_to_all | solution.py:20
  109.9 1204.1 %reduce-scatter.5.cloned.1.call-start = ((), (), s32[]{:S(2)}) async-start(), calls=%async_computation.6 | async-start | bytes 2621440 | tf_op jit(solution)/shard_map/reduce_scatter | solution.py:27
  1261.0 84.3 %reduce-scatter.3.cloned.1.call-start = ((), (), s32[]{:S(2)}) async-start(), calls=%async_computation.5 | async-start | bytes 2621440 | tf_op jit(solution)/shard_map/reduce_scatter | solution.py:26
Sparse Core Ops, SparseCore 0:
  97.4 1110.6 all-gather.1
  1261.1 31.1 reduce-scatter.4
  1314.1 31.1 reduce-scatter.2
where the time goes:
time: 1350 us
  waiting for transfers between devices  1130 us (84%)
  matrix products  106 us (8%)
  blocking collectives  86.2 us (6%)
  between operations  13.8 us (1%)
    all_gather x1, waiting for transfers between devices, shards(): every_orb = lax.all_gather(mine_orb, 'row', axis=0, tiled=True)  1100 us
    dot_general x2, matrix products, product(): lax.dot_general(left, right, (((1,), (1,)), ((), ())), precision=lax.Prec...  106 us
    all_to_all x1, blocking collectives, shards(): lax.all_to_all(orbitals, 'col', split_axis=1, concat_axis=0, tiled=True)  86.2 us
    reduce_scatter x1, waiting for transfers between devices, shards(): lax.psum_scatter(ham_part, 'col', scatter_dimension=0, tiled=True)  31.3 us
  transfers between devices with their start and end apart: 4, of which 2 were waited for; matrix products, arithmetic and copies ran while one was open for 8% of the time, Pallas kernels for 0%

commit v1 on v0

--- a/solution.py
+++ b/solution.py
@@ -9,7 +9,7 @@
         left,
         right,
         (((1,), (1,)), ((), ())),
-        precision=lax.Precision.HIGHEST,
+        precision=lax.Precision.HIGH,
         preferred_element_type=jnp.float32,
     )
 

time: 1350 us -> 1310 us (0.970)
  matrix products: 106 us -> 64.7 us
    dot_general x2, matrix products: 106 us -> 64.7 us  [product(): lax.dot_general(left, right, (((1,), (1,)), ((), ())), precision=lax.Prec...]
  transfers between devices with their start and end apart: 4 -> 4, of which waited for: 2 -> 2; matrix products, arithmetic and copies ran while one was open for 8% -> 5% of each run, Pallas kernels for 0% -> 0%
where the time goes in v1:
time: 1310 us
  waiting for transfers between devices  1130 us (86%)
  blocking collectives  86.2 us (7%)
  matrix products  64.7 us (5%)
  between operations  13.8 us (1%)
    all_gather x1, waiting for transfers between devices, shards(): every_orb = lax.all_gather(mine_orb, 'row', axis=0, tiled=True)  1100 us
    all_to_all x1, blocking collectives, shards(): lax.all_to_all(orbitals, 'col', split_axis=1, concat_axis=0, tiled=True)  86.2 us
    dot_general x2, matrix products, product(): lax.dot_general(left, right, (((1,), (1,)), ((), ())), precision=lax.Prec...  64.7 us
    reduce_scatter x1, waiting for transfers between devices, shards(): lax.psum_scatter(ham_part, 'col', scatter_dimension=0, tiled=True)  32.6 us
  transfers between devices with their start and end apart: 4, of which 2 were waited for; matrix products, arithmetic and copies ran while one was open for 5% of the time, Pallas kernels for 0%

profile of v1, /device:TPU:0, one launch (start us, length us, event | category | flops | bytes accessed | tf_op | source)
XLA Modules:
  0.0 1312.4 jit_solution(1408428525914762952)
XLA Ops:
  7.2 0.0 all-gather.2.cloned.1.call-start
  7.2 3.9 copy.13
  11.1 86.2 %all_to_all.38 = f32[64,4,7168]{2,0,1:T(8,128)} all-to-all(f32[64,4,7168]{2,0,1:T(8,128)S(1)} %bitcast.21), channel_id=1, replica_groups=mesh['row'=8,'col'=4] {'col'}, dimensions={1} | all-to-all | bytes 14680064 | tf_op jit(solution)/shard_map/all_to_all | solution.py:19
  97.3 0.0 all-gather.2.cloned.1.call-update
  97.3 6.9 copy.12
  104.3 5.6 all-to-all-start.1
  109.9 0.0 reduce-scatter.5.cloned.1.call-start
  109.9 1098.2 %all-gather.2.cloned.1.call-done = f32[2048,7168]{1,0:T(8,128)} async-done(((f32[256,7168]{1,0:T(8,128)}), f32[2048,7168]{1,0:T(8,128)}) %all-gather.2.cloned.1.call-update) | async-done | bytes 58720272 | tf_op jit(solution)/shard_map/all_gather | solution.py:22
  1208.2 32.0 %fusion.1 = f32[2048,256]{1,0:T(8,128)} fusion(f32[2048,7168]{1,0:T(8,128)} %all-gather.2.cloned.1.call-done, f32[256,7168]{1,0:T(8,128)} %bitcast.19), kind=kOutput, calls=%fused_computation.3 | convolution fusion | flops 22548578304 | bytes 68157440 | tf_op jit(solution)/shard_map/dot_general | solution.py:8
  1240.2 0.0 reduce-scatter.5.cloned.1.call-update
  1240.2 0.2 reduce-scatter.3.cloned.1.call-start
  1240.4 0.0 all-to-all-done.1
  1240.5 32.7 %fusion = f32[2048,256]{1,0:T(8,128)} fusion(f32[2048,7168]{1,0:T(8,128)} %all-gather.2.cloned.1.call-done, f32[256,7168]{1,0:T(8,128)} %bitcast.3), kind=kOutput, calls=%fused_computation.2 | convolution fusion | flops 22548578304 | bytes 68157440 | tf_op jit(solution)/shard_map/dot_general | solution.py:8
  1273.2 0.0 reduce-scatter.3.cloned.1.call-update
  1273.2 0.0 reduce-scatter.5.cloned.1.call-done
  1273.2 32.6 %reduce-scatter.3.cloned.1.call-done = f32[512,256]{1,0:T(8,128)} async-done(((f32[2048,256]{1,0:T(8,128)}), f32[512,256]{1,0:T(8,128)}) %reduce-scatter.3.cloned.1.call-update) | async-done | bytes 524304 | tf_op jit(solution)/shard_map/reduce_scatter | solution.py:26
Async XLA Ops:
  7.2 1201.0 %all-gather.2.cloned.1.call-start = ((), (), s32[]{:S(2)}) async-start(), calls=%async_computation.4 | async-start | bytes 66060288 | tf_op jit(solution)/shard_map/all_gather | solution.py:22
  104.3 1136.2 %all-to-all-start.1 = ((f32[64,4,7168]{2,0,1:T(8,128)}), f32[64,4,7168]{2,0,1:T(8,128)}, u32[]{:S(2)}, u32[]{:S(2)}) async-start(f32[64,4,7168]{2,0,1:T(8,128)} %bitcast.20), calls=%async_computation.1 | async-start | bytes 14680064 | tf_op jit(solution)/shard_map/all_to_all | solution.py:20
  109.9 1163.3 %reduce-scatter.5.cloned.1.call-start = ((), (), s32[]{:S(2)}) async-start(), calls=%async_computation.6 | async-start | bytes 2621440 | tf_op jit(solution)/shard_map/reduce_scatter | solution.py:27
  1240.2 65.6 %reduce-scatter.3.cloned.1.call-start = ((), (), s32[]{:S(2)}) async-start(), calls=%async_computation.5 | async-start | bytes 2621440 | tf_op jit(solution)/shard_map/reduce_scatter | solution.py:26
Sparse Core Ops, SparseCore 0:
  97.4 1110.6 all-gather.1
  1240.3 31.1 reduce-scatter.4
  1274.6 31.1 reduce-scatter.2
